TPU v7x, 256 devices: a whole 4x4x8 slice. The times are simulated.
256 devices in a mesh: rep: 32 (over x_hi, z, core), tp: 8 (over x_lo, y).
Axes of the slice: x: 4 (x_hi: 2, x_lo: 2; x = x_hi * 2 + x_lo), y: 4, z: 8, core: 2. Of those that a mesh axis runs over, the one named last changes fastest.
Arguments:
- hidden: bfloat16 [4, 2048, 8192], P(None, 'rep', 'tp'), may hold values from -6 to 6
- query_base: bfloat16 [4, 2048, 8192], P(None, 'rep', 'tp'), may hold values from -13 to 13
- kv_base: bfloat16 [4, 2048, 2, 1024], P(None, 'rep', None, 'tp'), may hold values from -6 to 6
- kv_cache: bfloat16 [2048, 128, 2, 1024], P('rep', None, None, 'tp'), may hold values from -13 to 13
- cache_lengths: int32 [2048], P('rep'), may hold values from 2 to 124
- adapter_ids: int32 [4, 2048], P(None, 'rep'), may hold values from 0 to 5, as said below
- migrating: int32 [4, 64], P(None, 'rep'), may hold values from 0 to 63, as said below
- pair_mask: int32 [4], replicated, may hold values from 1 to 16, as said below
- owners: int32 [4], replicated, may hold values from 0 to 31, as said below
- pool_down: bfloat16 [2, 2, 64, 8192], P(None, None, None, 'tp'), may hold values from -0.0625 to 0.0625
- pool_upq: bfloat16 [2, 64, 8192], P(None, None, 'tp'), may hold values from -0.75 to 0.75
- pool_upv: bfloat16 [2, 64, 1024], P(None, None, 'tp'), may hold values from -0.75 to 0.75
- store_down: bfloat16 [32, 2, 64, 8192], P('rep', None, None, 'tp'), may hold values from -0.0625 to 0.0625
- store_upq: bfloat16 [32, 64, 8192], P('rep', None, 'tp'), may hold values from -0.75 to 0.75
- store_upv: bfloat16 [32, 64, 1024], P('rep', None, 'tp'), may hold values from -0.75 to 0.75
Outputs:
- attention: bfloat16 [4, 2048, 8192], P(None, 'rep', 'tp')
Inputs may be any that keep to these rules, and one draw needn't show every extreme that they name: The 4 owners are distinct replicas. `migrating`: at one step the 2 entries of one replica are distinct slots. `adapter_ids`: at step s every entry is at most 2 + s. `pair_mask`: every entry is a power of two.
All inputs are finite; a program needn't handle non-finite values.
Results may differ from a plain program's by a relative error of at most 0.0064.
Values may be sent and summed in bfloat16 or wider, within the bound.
No kernel may reach another device: no remote copies, remote signals or barrier semaphores. Data moves between devices by JAX's collectives and lax.ppermute only.
A program may use at most 128 MiB of HBM per device.

v0:
```python
import math
import jax
import jax.numpy as jnp
from jax import lax
from jax.sharding import PartitionSpec as P

HD = 128
POOL = 2
STEPS = 4


def from_root(value, axis, source):
    kept = jnp.where(lax.axis_index(axis) == source, value, 0).astype(value.dtype)
    return lax.psum(kept, axis)


def attend(query_rows, kv_rows, lengths, head_dim):
    req_count = kv_rows.shape[0]
    ctx_len = kv_rows.shape[1]
    kv_local = kv_rows.shape[3] // head_dim
    group_size = query_rows.shape[1] // (kv_local * head_dim)
    heads_q = query_rows.reshape(req_count, kv_local, group_size, head_dim)
    key_rows = kv_rows[:, :, 0].reshape(req_count, ctx_len, kv_local, head_dim)
    value_rows = kv_rows[:, :, 1].reshape(req_count, ctx_len, kv_local, head_dim)
    scores = jnp.einsum(
        "rkgd,rckd->rkgc", heads_q, key_rows, preferred_element_type=jnp.float32
    ) / math.sqrt(head_dim)
    valid_mask = jnp.arange(ctx_len)[None, :] <= lengths[:, None]
    scores = jnp.where(valid_mask[:, None, None, :], scores, -1e30)
    row_peak = jnp.max(scores, axis=-1, keepdims=True)
    exp_scores = jnp.exp(scores - row_peak)
    weights = (exp_scores / jnp.sum(exp_scores, axis=-1, keepdims=True)).astype(jnp.bfloat16)
    mixed_out = jnp.einsum(
        "rkgc,rckd->rkgd", weights, value_rows, preferred_element_type=jnp.float32
    )
    return mixed_out.astype(jnp.bfloat16).reshape(req_count, -1)


def local(
    hidden,
    query_base,
    kv_base,
    kv_cache,
    cache_lengths,
    adapter_ids,
    migrating,
    pair_mask,
    owners,
    pool_down,
    pool_upq,
    pool_upv,
    store_down,
    store_upq,
    store_upv,
):
    slots_all = POOL + STEPS
    rep_index = lax.axis_index("rep")
    down_all = jnp.concatenate(
        [pool_down, jnp.zeros((STEPS,) + pool_down.shape[1:], jnp.bfloat16)], axis=0
    )
    upq_all = jnp.concatenate(
        [pool_upq, jnp.zeros((STEPS,) + pool_upq.shape[1:], jnp.bfloat16)], axis=0
    )
    upv_all = jnp.concatenate(
        [pool_upv, jnp.zeros((STEPS,) + pool_upv.shape[1:], jnp.bfloat16)], axis=0
    )
    kv_state = kv_cache
    lengths = cache_lengths
    req_count = kv_cache.shape[0]
    outputs = []
    for step_num in range(STEPS):
        arrived = (
            from_root(store_down[0], "rep", owners[step_num]),
            from_root(store_upq[0], "rep", owners[step_num]),
            from_root(store_upv[0], "rep", owners[step_num]),
        )
        down_all = down_all.at[POOL + step_num].set(arrived[0])
        upq_all = upq_all.at[POOL + step_num].set(arrived[1])
        upv_all = upv_all.at[POOL + step_num].set(arrived[2])
        slot_ids = migrating[step_num]
        moving = kv_state[slot_ids]
        moving_len = lengths[slot_ids].astype(jnp.bfloat16)
        replicas = lax.axis_size("rep")
        partner = jnp.bitwise_xor(rep_index, pair_mask[step_num])
        chosen_slot = jnp.arange(replicas) == partner
        send_rows = jnp.where(
            chosen_slot[:, None, None, None, None], moving[None], jnp.zeros((), jnp.bfloat16)
        )
        send_len = jnp.where(chosen_slot[:, None], moving_len[None], jnp.zeros((), jnp.bfloat16))
        got_rows, got_len = (
            lax.all_to_all(send_rows, "rep", split_axis=0, concat_axis=0, tiled=True),
            lax.all_to_all(send_len, "rep", split_axis=0, concat_axis=0, tiled=True),
        )
        moving = got_rows[partner]
        moving_len = got_len[partner]
        kv_state = kv_state.at[slot_ids].set(moving)
        lengths = lengths.at[slot_ids].set(moving_len.astype(jnp.int32))
        tokens = hidden[step_num]
        partial_sum = jnp.einsum(
            "rd,apkd->rapk", tokens, down_all, preferred_element_type=jnp.float32
        )
        picker = (adapter_ids[step_num][:, None] == jnp.arange(slots_all)[None, :]).astype(
            jnp.float32
        )
        summed = lax.psum(partial_sum, "tp")
        low_rank = jnp.sum(picker[:, :, None, None] * summed, axis=1)
        low_rank = low_rank.astype(jnp.bfloat16)
        spread = picker.astype(jnp.bfloat16)[:, :, None, None] * low_rank[:, None]
        spread_q = spread[:, :, 0].reshape(req_count, -1)
        spread_v = spread[:, :, 1].reshape(req_count, -1)
        delta_q = jnp.dot(
            spread_q, upq_all.reshape(-1, upq_all.shape[2]), preferred_element_type=jnp.float32
        )
        delta_v = jnp.dot(
            spread_v, upv_all.reshape(-1, upv_all.shape[2]), preferred_element_type=jnp.float32
        )
        query_rows = (query_base[step_num].astype(jnp.float32) + delta_q).astype(jnp.bfloat16)
        new_value = (kv_base[step_num][:, 1].astype(jnp.float32) + delta_v).astype(jnp.bfloat16)
        fresh_rows = jnp.stack([kv_base[step_num][:, 0], new_value], axis=1)
        kv_state = kv_state.at[jnp.arange(req_count), lengths].set(fresh_rows)
        outputs.append(attend(query_rows, kv_state, lengths, HD))
        lengths = lengths + 1
    return jnp.stack(outputs, axis=0)


def solution(mesh):
    return jax.shard_map(
        local,
        mesh=mesh,
        in_specs=(
            P(None, "rep", "tp"),
            P(None, "rep", "tp"),
            P(None, "rep", None, "tp"),
            P("rep", None, None, "tp"),
            P("rep"),
            P(None, "rep"),
            P(None, "rep"),
            P(),
            P(),
            P(None, None, None, "tp"),
            P(None, None, "tp"),
            P(None, None, "tp"),
            P("rep", None, None, "tp"),
            P("rep", None, "tp"),
            P("rep", None, "tp"),
        ),
        out_specs=P(None, "rep", "tp"),
        check_vma=False,
    )
```

profile of v0, /device:TPU:1, one launch (start us, length us, event | category | flops | bytes accessed | tf_op | source)
XLA Modules:
  0.0 1123.3 jit_solution(8069463580083351117)
XLA Ops:
  7.2 10.3 copy.207
  20.5 12.6 %all-to-all-start = ((bf16[32,1,2]{2,1,0:T(2,128)(2,1)}), bf16[32,1,2]{2,1,0:T(2,128)(2,1)S(1)}, u32[]{:S(2)}, u32[]{:S(2)}) async-start(bf16[32,1,2]{2,1,0:T(2,128)(2,1)} %broadcast_select_fusion.15), calls=%async_computation | async-start | bytes 32768 | tf_op jit(solution)/shard_map/all_to_all | solution.py:92
  33.7 3.0 gather_fusion.1
  36.8 5.6 all-to-all-done
  44.3 4.3 all-to-all-start.2
  48.6 2.3 broadcast_select_fusion.3
  51.0 7.1 all-to-all-done.2
  58.0 5.2 all-to-all-start.1
  70.4 287.7 %all-reduce.14.cloned.1.call-done = (bf16[1,2,64,1024]{3,2,1,0:T(8,128)(2,1)}, bf16[1,2,64,1024]{3,2,1,0:T(8,128)(2,1)}, bf16[1,2,64,1024]{3,2,1,0:T(8,128)(2,1)...) async-done(((bf16[1,2,64,1024]{3,2,1,0:T(8,128)(2,1)}, ...) | async-done | bytes 1572880 | tf_op jit(solution)/shard_map/psum | solution.py:14
  362.8 1.3 convolution_bitcast_fusion.1
  367.5 227.4 %all-reduce.12.cloned.1.call-done = (bf16[1,64,128]{2,1,0:T(8,128)(2,1)}, bf16[1,64,128]{2,1,0:T(8,128)(2,1)}, bf16[1,64,128]{2,1,0:T(8,128)(2,1)}, bf16[1,64,128]{2,1,0:T(8,128)(2,1)}) async-done(((bf16[1,64,128]{2,1,0:T(8,128)(2,1)}, bf16[1,64,128]{2,1,0:T(8,128)(2,1)}, bf16[1,64,128]{2,1,0:T(8,128)(2,1)}, bf16[1,64,128]{2,1,0:T(8,128)(2,1)}), (bf16[1,64,128]{2,1,0:T(8,128)(2,1)}, ...) | async-done | bytes 65552 | tf_op jit(solution)/shard_map/psum | solution.py:14
  595.6 79.9 %all-reduce.10.cloned.1.call-done = (f32[64,6,2,64]{0,3,2,1:T(8,128)}, f32[64,6,2,64]{0,3,2,1:T(8,128)}, f32[64,6,2,64]{0,3,2,1:T(8,128)}, f32[64,6,2,64]{0,3,2,1:T(8,128)}) async-done(((f32[64,6,2,64]{0,3,2,1:T(8,128)}, f32[64,6,2,64]{0,3,2,1:T(8,128)}, f32[64,6,2,64]{0,3,2,1:T(8,128)}, f32[64,6,2,64]{0,3,2,1:T(8,128)}), (f32[64,6,2,64]{0,3,2,1:T(8,128)}, f32[64,6,2,64]{0,3,2,1:T(8,128)}, ...) | async-done | bytes 786448 | tf_op jit(solution)/shard_map/psum | solution.py:105
  677.3 14.0 %all-to-all-start.4 = ((bf16[32,1,2]{2,1,0:T(2,128)(2,1)}), bf16[32,1,2]{2,1,0:T(2,128)(2,1)S(1)}, u32[]{:S(2)}, u32[]{:S(2)}) async-start(bf16[32,1,2]{2,1,0:T(2,128)(2,1)} %broadcast_select_fusion.13), calls=%async_computation.4 | async-start | bytes 32768 | tf_op jit(solution)/shard_map/all_to_all | solution.py:92
  692.4 2.2 scatter_fusion.1
  694.6 8.0 scatter_fusion.2
  702.5 3.0 gather_fusion.3
  705.6 2.3 broadcast_select_fusion.2
  707.9 10.1 all-to-all-start.3
  721.4 5.3 copy.75
  726.7 87.4 %all-to-all-done.3 = bf16[32,2,128,2,128]{4,2,3,1,0:T(8,128)(2,1)} async-done(((bf16[32,2,128,2,128]{4,2,3,1,0:T(8,128)(2,1)}), bf16[32,2,128,2,128]{4,2,3,1,0:T(8,128)(2,1)}, u32[]{:S(2)}, u32[]{:S(2)}) %all-to-all-start.3) | async-done | bytes 4194336 | tf_op jit(solution)/shard_map/all_to_all | solution.py:91
  814.2 7.1 all-to-all-start.6
  822.2 2.1 scatter_fusion.4
  824.2 8.5 copy.77
  832.7 8.0 scatter_fusion.5
  840.7 3.0 gather_fusion.5
  843.7 2.3 broadcast_select_fusion.1
  846.0 10.1 all-to-all-start.5
  858.4 5.3 copy.84
  863.7 88.7 %all-to-all-done.5 = bf16[32,2,128,2,128]{4,2,3,1,0:T(8,128)(2,1)} async-done(((bf16[32,2,128,2,128]{4,2,3,1,0:T(8,128)(2,1)}), bf16[32,2,128,2,128]{4,2,3,1,0:T(8,128)(2,1)}, u32[]{:S(2)}, u32[]{:S(2)}) %all-to-all-start.5) | async-done | bytes 4194336 | tf_op jit(solution)/shard_map/all_to_all | solution.py:91
  953.3 2.1 scatter_fusion.7
  955.4 8.5 copy.86
  963.9 7.9 scatter_fusion.8
  971.8 3.0 gather_fusion.7
  974.8 2.3 broadcast_select_fusion
  977.2 7.8 all-to-all-start.7
  987.6 9.9 fusion.93
  999.0 3.1 fusion.32
  1002.2 10.0 fusion.94
  1013.6 3.1 fusion.33
  1016.8 5.4 copy.93
  1022.2 6.8 fusion.95
  1030.4 3.1 fusion.34
  1033.6 47.4 %all-to-all-done.7 = bf16[32,2,128,2,128]{4,2,3,1,0:T(8,128)(2,1)} async-done(((bf16[32,2,128,2,128]{4,2,3,1,0:T(8,128)(2,1)}), bf16[32,2,128,2,128]{4,2,3,1,0:T(8,128)(2,1)}, u32[]{:S(2)}, u32[]{:S(2)}) %all-to-all-start.7) | async-done | bytes 4194336 | tf_op jit(solution)/shard_map/all_to_all | solution.py:91
  1081.9 2.3 scatter_fusion.10
  1084.3 8.5 copy.95
  1092.8 8.0 scatter_fusion.11
  1100.8 10.0 fusion.96
  1112.2 3.1 fusion.35
  (205 shorter events, 37.1 us)
Async XLA Ops:
  7.2 10.4 copy-start.22
  7.2 11.7 %copy-start.17 = (s32[4,2]{0,1:T(2,128)S(1)}, s32[4,2]{0,1:T(2,128)}, u32[]{:S(2)}) copy-start(s32[4,2]{0,1:T(2,128)} %param.45) | copy-start | bytes 100
  20.5 21.9 %all-to-all-start = ((bf16[32,1,2]{2,1,0:T(2,128)(2,1)}), bf16[32,1,2]{2,1,0:T(2,128)(2,1)S(1)}, u32[]{:S(2)}, u32[]{:S(2)}) async-start(bf16[32,1,2]{2,1,0:T(2,128)(2,1)} %broadcast_select_fusion.15), calls=%async_computation | async-start | bytes 32768 | tf_op jit(solution)/shard_map/all_to_all | solution.py:92
  44.3 13.7 %all-to-all-start.2 = ((bf16[32,1,2]{2,1,0:T(2,128)(2,1)}), bf16[32,1,2]{2,1,0:T(2,128)(2,1)S(1)}, u32[]{:S(2)}, u32[]{:S(2)}) async-start(bf16[32,1,2]{2,1,0:T(2,128)(2,1)} %broadcast_select_fusion.14), calls=%async_computation.2 | async-start | bytes 32768 | tf_op jit(solution)/shard_map/all_to_all | solution.py:92
  50.9 12.4 %copy-start.23 = (s32[4]{0:T(128)S(1)}, s32[4]{0:T(128)}, u32[]{:S(2)}) copy-start(s32[4]{0:T(128)} %param.47) | copy-start | bytes 52
  50.9 15.6 %copy-start.10 = (bf16[1,64,1024]{2,1,0:T(8,128)(2,1)S(1)}, bf16[1,64,1024]{2,1,0:T(8,128)(2,1)}, u32[]{:S(2)}) copy-start(bf16[1,64,1024]{2,1,0:T(8,128)(2,1)} %param.52) | copy-start | bytes 393220
  50.9 16.5 %copy-start.6 = (bf16[1,2,64,1024]{3,2,1,0:T(8,128)(2,1)S(1)}, bf16[1,2,64,1024]{3,2,1,0:T(8,128)(2,1)}, u32[]{:S(2)}) copy-start(bf16[1,2,64,1024]{3,2,1,0:T(8,128)(2,1)} %param.51) | copy-start | bytes 786436
  50.9 17.5 %copy-start.21 = (bf16[1,64,128]{2,1,0:T(8,128)(2,1)S(1)}, bf16[1,64,128]{2,1,0:T(8,128)(2,1)}, u32[]{:S(2)}) copy-start(bf16[1,64,128]{2,1,0:T(8,128)(2,1)} %param.53) | copy-start | bytes 49156
  50.9 18.3 %copy-start.24 = (s32[4,64]{1,0:T(4,128)S(1)}, s32[4,64]{1,0:T(4,128)}, u32[]{:S(2)}) copy-start(s32[4,64]{1,0:T(4,128)} %param.44) | copy-start | bytes 3076
  51.0 18.4 %copy-start.1 = (bf16[2,2,64,1024]{3,2,1,0:T(8,128)(2,1)S(1)}, bf16[2,2,64,1024]{3,2,1,0:T(8,128)(2,1)}, u32[]{:S(2)}) copy-start(bf16[2,2,64,1024]{3,2,1,0:T(8,128)(2,1)} %param.48) | copy-start | bytes 1572868
  58.0 619.3 %all-to-all-start.1 = ((bf16[32,2,128,2,128]{4,2,3,1,0:T(8,128)(2,1)}), bf16[32,2,128,2,128]{4,2,3,1,0:T(8,128)(2,1)}, u32[]{:S(2)}, u32[]{:S(2)}) async-start(bf16[32,2,128,2,128]{4,2,3,1,0:T(8,128)(2,1)} %broadcast_select_fusion.3), calls=%async_computation.1 | async-start | bytes 8388608 | tf_op jit(solution)/shard_map/all_to_all | solution.py:91
  63.3 6.3 copy-start.16
  63.3 6.3 copy-start.11
  63.3 295.9 %copy-start.2 = (bf16[4,64,1024]{2,1,0:T(8,128)(2,1)S(1)}, bf16[4,64,1024]{2,1,0:T(8,128)(2,1)}, u32[]{:S(2)}) copy-start(bf16[4,64,1024]{2,1,0:T(8,128)(2,1)} %param.39) | copy-start | bytes 1572868
  63.3 294.9 %all-reduce.14.cloned.1.call-start = ((), (), s32[]{:S(2)}) async-start(), calls=%async_computation.10 | async-start | bytes 3145728 | tf_op jit(solution)/shard_map/psum | solution.py:14
  68.4 526.5 %all-reduce.12.cloned.1.call-start = ((), (), s32[]{:S(2)}) async-start(), calls=%async_computation.9 | async-start | bytes 131072 | tf_op jit(solution)/shard_map/psum | solution.py:14
  69.2 606.3 %all-reduce.10.cloned.1.call-start = ((), (), s32[]{:S(2)}) async-start(), calls=%async_computation.8 | async-start | bytes 3145728 | tf_op jit(solution)/shard_map/psum | solution.py:105
  358.2 4.7 copy-start.8
  358.2 6.0 copy-start.7
  677.3 30.6 %all-to-all-start.4 = ((bf16[32,1,2]{2,1,0:T(2,128)(2,1)}), bf16[32,1,2]{2,1,0:T(2,128)(2,1)S(1)}, u32[]{:S(2)}, u32[]{:S(2)}) async-start(bf16[32,1,2]{2,1,0:T(2,128)(2,1)} %broadcast_select_fusion.13), calls=%async_computation.4 | async-start | bytes 32768 | tf_op jit(solution)/shard_map/all_to_all | solution.py:92
  707.9 13.3 %copy-start.20 = (bf16[1,64,128]{2,1,0:T(8,128)(2,1)S(1)}, bf16[1,64,128]{2,1,0:T(8,128)(2,1)}, u32[]{:S(2)}) copy-start(bf16[1,64,128]{2,1,0:T(8,128)(2,1)} %get-tuple-element.158) | copy-start | bytes 49156
  707.9 106.3 %all-to-all-start.3 = ((bf16[32,2,128,2,128]{4,2,3,1,0:T(8,128)(2,1)}), bf16[32,2,128,2,128]{4,2,3,1,0:T(8,128)(2,1)}, u32[]{:S(2)}, u32[]{:S(2)}) async-start(bf16[32,2,128,2,128]{4,2,3,1,0:T(8,128)(2,1)} %broadcast_select_fusion.2), calls=%async_computation.3 | async-start | bytes 8388608 | tf_op jit(solution)/shard_map/all_to_all | solution.py:91
  814.2 31.9 %all-to-all-start.6 = ((bf16[32,1,2]{2,1,0:T(2,128)(2,1)}), bf16[32,1,2]{2,1,0:T(2,128)(2,1)S(1)}, u32[]{:S(2)}, u32[]{:S(2)}) async-start(bf16[32,1,2]{2,1,0:T(2,128)(2,1)} %broadcast_select_fusion.12), calls=%async_computation.6 | async-start | bytes 32768 | tf_op jit(solution)/shard_map/all_to_all | solution.py:92
  846.0 10.1 copy-start.9
  846.0 11.6 %copy-start.4 = (f32[64,6,2,64]{0,3,2,1:T(8,128)S(1)}, f32[64,6,2,64]{0,3,2,1:T(8,128)}, u32[]{:S(2)}) copy-start(f32[64,6,2,64]{0,3,2,1:T(8,128)} %get-tuple-element.155) | copy-start | bytes 589828
  846.0 11.6 %copy-start.5 = (f32[64,6,2,64]{0,3,2,1:T(8,128)S(1)}, f32[64,6,2,64]{0,3,2,1:T(8,128)}, u32[]{:S(2)}) copy-start(f32[64,6,2,64]{0,3,2,1:T(8,128)} %get-tuple-element.156) | copy-start | bytes 589828
  846.0 106.3 %all-to-all-start.5 = ((bf16[32,2,128,2,128]{4,2,3,1,0:T(8,128)(2,1)}), bf16[32,2,128,2,128]{4,2,3,1,0:T(8,128)(2,1)}, u32[]{:S(2)}, u32[]{:S(2)}) async-start(bf16[32,2,128,2,128]{4,2,3,1,0:T(8,128)(2,1)} %broadcast_select_fusion.1), calls=%async_computation.5 | async-start | bytes 8388608 | tf_op jit(solution)/shard_map/all_to_all | solution.py:91
  856.2 2.0 copy-start.19
  977.2 7.9 copy-start.15
  977.2 8.1 copy-start.3
  977.2 8.6 copy-start.14
  977.2 9.0 copy-start.13
  977.2 103.9 %all-to-all-start.7 = ((bf16[32,2,128,2,128]{4,2,3,1,0:T(8,128)(2,1)}), bf16[32,2,128,2,128]{4,2,3,1,0:T(8,128)(2,1)}, u32[]{:S(2)}, u32[]{:S(2)}) async-start(bf16[32,2,128,2,128]{4,2,3,1,0:T(8,128)(2,1)} %broadcast_select_fusion), calls=%async_computation.7 | async-start | bytes 8388608 | tf_op jit(solution)/shard_map/all_to_all | solution.py:91
  985.0 2.0 copy-start.18
  985.0 2.3 copy-start.12
  1016.8 5.4 copy-start
Sparse Core Ops, SparseCore 0:
  68.5 289.5 all-reduce.13
  361.1 233.7 all-reduce.11
  597.8 77.6 all-reduce.9
where the time goes:
time: 1130 us; the launch traced here: 1120 us
  waiting for transfers between devices  831 us (74%)
  local copies, waits for them, and re-layouts  158 us (14%)
  starting transfers between devices  71.2 us (6%)
  matrix products  24.1 us (2%)
  between operations  19.8 us (2%)
  other arithmetic  18.8 us (2%)
    psum x2, waiting for transfers between devices, from_root(): return lax.psum(kept, axis)  515 us
    all_to_all x4, waiting for transfers between devices, local(): lax.all_to_all(send_rows, 'rep', split_axis=0, concat_axis=0, tiled=True)  224 us
    psum x1, waiting for transfers between devices, local(): summed = lax.psum(partial_sum, 'tp')  79.9 us
    scatter x7, local copies, waits for them, and re-layouts, local(): kv_state = kv_state.at[jnp.arange(req_count), lengths].set(fresh_rows)  47.9 us
    all_to_all x4, starting transfers between devices, local(): lax.all_to_all(send_len, 'rep', split_axis=0, concat_axis=0, tiled=True)  37.9 us
    slice x4, local copies, waits for them, and re-layouts, attend(): key_rows = kv_rows[:, :, 0].reshape(req_count, ctx_len, kv_local, head_dim)  36.7 us
    scatter x7, local copies, waits for them, and re-layouts, local(): kv_state = kv_state.at[slot_ids].set(moving)  34.2 us
    all_to_all x4, starting transfers between devices, local(): lax.all_to_all(send_rows, 'rep', split_axis=0, concat_axis=0, tiled=True)  33.2 us
  transfers between devices with their start and end apart: 11, of which 8 were waited for; matrix products, arithmetic and copies ran while one was open for 11% of the time, Pallas kernels for 0%

commit v1 on v0

--- a/solution.py
+++ b/solution.py
@@ -102,7 +102,8 @@
         picker = (adapter_ids[step_num][:, None] == jnp.arange(slots_all)[None, :]).astype(
             jnp.float32
         )
-        summed = lax.psum(partial_sum, "tp")
+        blocks = lax.all_gather(partial_sum, "tp")
+        summed = jnp.sum(blocks, axis=0)
         low_rank = jnp.sum(picker[:, :, None, None] * summed, axis=1)
         low_rank = low_rank.astype(jnp.bfloat16)
         spread = picker.astype(jnp.bfloat16)[:, :, None, None] * low_rank[:, None]

time: 1130 us -> 1100 us (0.973)
  waiting for transfers between devices: 831 us -> 774 us
  other arithmetic: 18.8 us -> 34.9 us
    all_gather x0 -> x4, waiting for transfers between devices: none -> 168 us  [local(): blocks = lax.all_gather(partial_sum, 'tp')]
    all_to_all x4, waiting for transfers between devices: 224 us -> 73.8 us  [local(): lax.all_to_all(send_rows, 'rep', split_axis=0, concat_axis=0, tiled=True)]
    psum x1 -> x0, waiting for transfers between devices: 79.9 us -> none  [local(): summed = lax.psum(partial_sum, 'tp')]
    reduce_sum x0 -> x4, other arithmetic: none -> 13.7 us  [local(): summed = jnp.sum(blocks, axis=0)]
  transfers between devices with their start and end apart: 11 -> 14, of which waited for: 8 -> 10; matrix products, arithmetic and copies ran while one was open for 11% -> 16% of each run, Pallas kernels for 0% -> 0%
where the time goes in v1:
time: 1100 us; the launch traced here: 1090 us
  waiting for transfers between devices  774 us (70%)
  local copies, waits for them, and re-layouts  168 us (15%)
  starting transfers between devices  70 us (6%)
  other arithmetic  34.9 us (3%)
  matrix products  21 us (2%)
  between operations  20.2 us (2%)
    psum x2, waiting for transfers between devices, from_root(): return lax.psum(kept, axis)  519 us
    all_gather x4, waiting for transfers between devices, local(): blocks = lax.all_gather(partial_sum, 'tp')  168 us
    all_to_all x4, waiting for transfers between devices, local(): lax.all_to_all(send_rows, 'rep', split_axis=0, concat_axis=0, tiled=True)  73.8 us
    scatter x7, local copies, waits for them, and re-layouts, local(): kv_state = kv_state.at[jnp.arange(req_count), lengths].set(fresh_rows)  48.2 us
    all_to_all x4, starting transfers between devices, local(): lax.all_to_all(send_len, 'rep', split_axis=0, concat_axis=0, tiled=True)  36.9 us
    slice x4, local copies, waits for them, and re-layouts, attend(): key_rows = kv_rows[:, :, 0].reshape(req_count, ctx_len, kv_local, head_dim)  36.8 us
    scatter x7, local copies, waits for them, and re-layouts, local(): kv_state = kv_state.at[slot_ids].set(moving)  34.2 us
    all_to_all x4, starting transfers between devices, local(): lax.all_to_all(send_rows, 'rep', split_axis=0, concat_axis=0, tiled=True)  32.9 us
  transfers between devices with their start and end apart: 14, of which 10 were waited for; matrix products, arithmetic and copies ran while one was open for 16% of the time, Pallas kernels for 0%

profile of v1, /device:TPU:1, one launch (start us, length us, event | category | flops | bytes accessed | tf_op | source)
XLA Modules:
  0.0 1088.5 jit_solution(3324481511305336987)
XLA Ops:
  7.2 10.4 copy.246
  20.5 12.6 %all-to-all-start = ((bf16[32,1,2]{2,1,0:T(2,128)(2,1)}), bf16[32,1,2]{2,1,0:T(2,128)(2,1)S(1)}, u32[]{:S(2)}, u32[]{:S(2)}) async-start(bf16[32,1,2]{2,1,0:T(2,128)(2,1)} %broadcast_select_fusion.15), calls=%async_computation | async-start | bytes 32768 | tf_op jit(solution)/shard_map/all_to_all | solution.py:92
  33.7 3.0 gather_fusion.1
  36.8 5.6 all-to-all-done
  44.3 4.3 all-to-all-start.2
  50.9 7.1 all-to-all-done.2
  58.0 5.2 all-to-all-start.1
  69.5 289.0 %all-reduce.10.cloned.1.call-done = (bf16[1,2,64,1024]{3,2,1,0:T(8,128)(2,1)}, bf16[1,2,64,1024]{3,2,1,0:T(8,128)(2,1)}, bf16[1,2,64,1024]{3,2,1,0:T(8,128)(2,1)...) async-done(((bf16[1,2,64,1024]{3,2,1,0:T(8,128)(2,1)}, ...) | async-done | bytes 1572880 | tf_op jit(solution)/shard_map/psum | solution.py:14
  365.2 230.0 %all-reduce.8.cloned.1.call-done = (bf16[1,64,128]{2,1,0:T(8,128)(2,1)}, bf16[1,64,128]{2,1,0:T(8,128)(2,1)}, bf16[1,64,128]{2,1,0:T(8,128)(2,1)}, bf16[1,64,128]{2,1,0:T(8,128)(2,1)}) async-done(((bf16[1,64,128]{2,1,0:T(8,128)(2,1)}, bf16[1,64,128]{2,1,0:T(8,128)(2,1)}, bf16[1,64,128]{2,1,0:T(8,128)(2,1)}, bf16[1,64,128]{2,1,0:T(8,128)(2,1)}), (bf16[1,64,128]{2,1,0:T(8,128)(2,1)}, ...) | async-done | bytes 65552 | tf_op jit(solution)/shard_map/psum | solution.py:14
  595.9 42.2 %all-gather.9.cloned.1.call-done = f32[512,6,2,64]{3,2,1,0:T(2,128)} async-done(((f32[64,6,2,64]{3,2,1,0:T(2,128)}), f32[512,6,2,64]{3,2,1,0:T(2,128)}) %all-gather.9.cloned.1.call-update) | async-done | bytes 1572880 | tf_op jit(solution)/shard_map/all_gather | solution.py:105
  638.1 3.4 reduce_sum.108
  642.5 12.6 %all-to-all-start.4 = ((bf16[32,1,2]{2,1,0:T(2,128)(2,1)}), bf16[32,1,2]{2,1,0:T(2,128)(2,1)S(1)}, u32[]{:S(2)}, u32[]{:S(2)}) async-start(bf16[32,1,2]{2,1,0:T(2,128)(2,1)} %broadcast_select_fusion.13), calls=%async_computation.4 | async-start | bytes 32768 | tf_op jit(solution)/shard_map/all_to_all | solution.py:92
  658.3 8.0 scatter_fusion.2
  666.3 3.0 gather_fusion.3
  669.3 2.3 broadcast_select_fusion.2
  671.6 10.0 all-to-all-start.3
  686.0 66.9 %all-gather.11.cloned.1.call-done = f32[512,6,2,64]{3,2,1,0:T(2,128)} async-done(((f32[64,6,2,64]{3,2,1,0:T(2,128)}), f32[512,6,2,64]{3,2,1,0:T(2,128)}) %all-gather.11.cloned.1.call-update) | async-done | bytes 1572880 | tf_op jit(solution)/shard_map/all_gather | solution.py:105
  752.9 3.4 reduce_sum.111
  757.9 5.3 copy.110
  763.2 14.7 %all-to-all-done.3 = bf16[32,2,128,2,128]{4,2,3,1,0:T(8,128)(2,1)} async-done(((bf16[32,2,128,2,128]{4,2,3,1,0:T(8,128)(2,1)}), bf16[32,2,128,2,128]{4,2,3,1,0:T(8,128)(2,1)}, u32[]{:S(2)}, u32[]{:S(2)}) %all-to-all-start.3) | async-done | bytes 4194336 | tf_op jit(solution)/shard_map/all_to_all | solution.py:91
  777.9 7.4 all-to-all-start.6
  788.3 8.5 copy.112
  796.8 8.0 scatter_fusion.5
  804.8 3.1 gather_fusion.5
  807.9 2.3 broadcast_select_fusion.1
  810.8 10.0 all-to-all-start.5
  832.8 59.1 %all-gather.13.cloned.1.call-done = f32[512,6,2,64]{3,2,1,0:T(2,128)} async-done(((f32[64,6,2,64]{3,2,1,0:T(2,128)}), f32[512,6,2,64]{3,2,1,0:T(2,128)}) %all-gather.13.cloned.1.call-update) | async-done | bytes 1572880 | tf_op jit(solution)/shard_map/all_gather | solution.py:105
  891.9 3.4 reduce_sum.114
  896.3 5.3 copy.121
  901.5 15.5 %all-to-all-done.5 = bf16[32,2,128,2,128]{4,2,3,1,0:T(8,128)(2,1)} async-done(((bf16[32,2,128,2,128]{4,2,3,1,0:T(8,128)(2,1)}), bf16[32,2,128,2,128]{4,2,3,1,0:T(8,128)(2,1)}, u32[]{:S(2)}, u32[]{:S(2)}) %all-to-all-start.5) | async-done | bytes 4194336 | tf_op jit(solution)/shard_map/all_to_all | solution.py:91
  920.0 8.6 copy.123
  928.6 8.1 scatter_fusion.8
  936.7 3.2 gather_fusion.7
  942.2 7.7 all-to-all-start.7
  951.4 3.4 reduce_sum.117
  956.3 10.0 fusion.93
  967.7 3.1 fusion.32
  970.9 10.0 fusion.94
  982.3 3.1 fusion.33
  985.5 5.4 copy.132
  990.9 6.8 fusion.95
  999.1 3.1 fusion.34
  1002.3 43.6 %all-to-all-done.7 = bf16[32,2,128,2,128]{4,2,3,1,0:T(8,128)(2,1)} async-done(((bf16[32,2,128,2,128]{4,2,3,1,0:T(8,128)(2,1)}), bf16[32,2,128,2,128]{4,2,3,1,0:T(8,128)(2,1)}, u32[]{:S(2)}, u32[]{:S(2)}) %all-to-all-start.7) | async-done | bytes 4194336 | tf_op jit(solution)/shard_map/all_to_all | solution.py:91
  1046.9 2.3 scatter_fusion.10
  1049.2 8.5 copy.134
  1057.7 8.2 scatter_fusion.11
  1065.9 10.1 fusion.96
  1077.3 3.1 fusion.35
  (282 shorter events, 58.5 us)
Async XLA Ops:
  7.2 10.4 copy-start.41
  7.2 11.7 %copy-start.29 = (s32[4,2]{0,1:T(2,128)S(1)}, s32[4,2]{0,1:T(2,128)}, u32[]{:S(2)}) copy-start(s32[4,2]{0,1:T(2,128)} %param.45) | copy-start | bytes 100
  19.1 344.1 %copy-start.37 = (s32[2]{0:T(128)}, s32[2]{0:T(128)S(1)}, u32[]{:S(2)}) copy-start(s32[2]{0:T(128)S(1)} %get-tuple-element.218) | copy-start | bytes 28
  20.5 21.9 %all-to-all-start = ((bf16[32,1,2]{2,1,0:T(2,128)(2,1)}), bf16[32,1,2]{2,1,0:T(2,128)(2,1)S(1)}, u32[]{:S(2)}, u32[]{:S(2)}) async-start(bf16[32,1,2]{2,1,0:T(2,128)(2,1)} %broadcast_select_fusion.15), calls=%async_computation | async-start | bytes 32768 | tf_op jit(solution)/shard_map/all_to_all | solution.py:92
  44.3 13.7 %all-to-all-start.2 = ((bf16[32,1,2]{2,1,0:T(2,128)(2,1)}), bf16[32,1,2]{2,1,0:T(2,128)(2,1)S(1)}, u32[]{:S(2)}, u32[]{:S(2)}) async-start(bf16[32,1,2]{2,1,0:T(2,128)(2,1)} %broadcast_select_fusion.14), calls=%async_computation.2 | async-start | bytes 32768 | tf_op jit(solution)/shard_map/all_to_all | solution.py:92
  50.9 12.4 %copy-start.42 = (s32[4]{0:T(128)S(1)}, s32[4]{0:T(128)}, u32[]{:S(2)}) copy-start(s32[4]{0:T(128)} %param.47) | copy-start | bytes 52
  50.9 15.7 %copy-start.9 = (bf16[1,64,1024]{2,1,0:T(8,128)(2,1)S(1)}, bf16[1,64,1024]{2,1,0:T(8,128)(2,1)}, u32[]{:S(2)}) copy-start(bf16[1,64,1024]{2,1,0:T(8,128)(2,1)} %param.52) | copy-start | bytes 393220
  50.9 16.5 %copy-start.5 = (bf16[1,2,64,1024]{3,2,1,0:T(8,128)(2,1)S(1)}, bf16[1,2,64,1024]{3,2,1,0:T(8,128)(2,1)}, u32[]{:S(2)}) copy-start(bf16[1,2,64,1024]{3,2,1,0:T(8,128)(2,1)} %param.51) | copy-start | bytes 786436
  50.9 17.6 %copy-start.34 = (bf16[1,64,128]{2,1,0:T(8,128)(2,1)S(1)}, bf16[1,64,128]{2,1,0:T(8,128)(2,1)}, u32[]{:S(2)}) copy-start(bf16[1,64,128]{2,1,0:T(8,128)(2,1)} %param.53) | copy-start | bytes 49156
  50.9 18.3 %copy-start.1 = (bf16[2,2,64,1024]{3,2,1,0:T(8,128)(2,1)S(1)}, bf16[2,2,64,1024]{3,2,1,0:T(8,128)(2,1)}, u32[]{:S(2)}) copy-start(bf16[2,2,64,1024]{3,2,1,0:T(8,128)(2,1)} %param.48) | copy-start | bytes 1572868
  58.0 584.4 %all-to-all-start.1 = ((bf16[32,2,128,2,128]{4,2,3,1,0:T(8,128)(2,1)}), bf16[32,2,128,2,128]{4,2,3,1,0:T(8,128)(2,1)}, u32[]{:S(2)}, u32[]{:S(2)}) async-start(bf16[32,2,128,2,128]{4,2,3,1,0:T(8,128)(2,1)} %broadcast_select_fusion.3), calls=%async_computation.1 | async-start | bytes 8388608 | tf_op jit(solution)/shard_map/all_to_all | solution.py:91
  63.3 296.2 %copy-start.2 = (bf16[4,64,1024]{2,1,0:T(8,128)(2,1)S(1)}, bf16[4,64,1024]{2,1,0:T(8,128)(2,1)}, u32[]{:S(2)}) copy-start(bf16[4,64,1024]{2,1,0:T(8,128)(2,1)} %param.39) | copy-start | bytes 1572868
  63.3 295.2 %all-reduce.10.cloned.1.call-start = ((), (), s32[]{:S(2)}) async-start(), calls=%async_computation.13 | async-start | bytes 3145728 | tf_op jit(solution)/shard_map/psum | solution.py:14
  67.5 293.5 %copy-start.49 = (s32[4,64]{1,0:T(4,128)S(1)}, s32[4,64]{1,0:T(4,128)}, u32[]{:S(2)}) copy-start(s32[4,64]{1,0:T(4,128)} %param.44) | copy-start | bytes 3076
  67.5 294.2 %copy-start.26 = (bf16[2,64,128]{2,1,0:T(8,128)(2,1)S(1)}, bf16[2,64,128]{2,1,0:T(8,128)(2,1)}, u32[]{:S(2)}) copy-start(bf16[2,64,128]{2,1,0:T(8,128)(2,1)} %param.50) | copy-start | bytes 98308
  68.4 293.3 %copy-start.10 = (bf16[4,64,2,128]{3,2,1,0:T(2,128)(2,1)S(1)}, bf16[4,64,2,128]{3,2,1,0:T(2,128)(2,1)}, u32[]{:S(2)}) copy-start(bf16[4,64,2,128]{3,2,1,0:T(2,128)(2,1)} %param.41) | copy-start | bytes 393220
  68.5 526.7 %all-reduce.8.cloned.1.call-start = ((), (), s32[]{:S(2)}) async-start(), calls=%async_computation.12 | async-start | bytes 131072 | tf_op jit(solution)/shard_map/psum | solution.py:14
  69.2 568.9 %all-gather.9.cloned.1.call-start = ((), (), s32[]{:S(2)}) async-start(), calls=%async_computation.8 | async-start | bytes 3538944 | tf_op jit(solution)/shard_map/all_gather | solution.py:105
  363.1 278.8 %copy-start.47 = (pred[32]{0:T(512)(128)(4,1)}, pred[32]{0:T(512)(128)(4,1)S(1)}, u32[]{:S(2)}) copy-start(pred[32]{0:T(512)(128)(4,1)S(1)} %iota_compare_fusion.10) | copy-start | bytes 100
  363.1 320.9 %copy-start.35 = (s32[2]{0:T(128)}, s32[2]{0:T(128)S(1)}, u32[]{:S(2)}) copy-start(s32[2]{0:T(128)S(1)} %get-tuple-element.220) | copy-start | bytes 28
  363.1 321.0 %copy-start.39 = (s32[2]{0:T(128)}, s32[2]{0:T(128)S(1)}, u32[]{:S(2)}) copy-start(s32[2]{0:T(128)S(1)} %get-tuple-element.219) | copy-start | bytes 28
  363.1 278.8 %copy-start.44 = (s32[1024]{0:T(1024)}, s32[1024]{0:T(1024)S(1)}, u32[]{:S(2)}) copy-start(s32[1024]{0:T(1024)S(1)} %pad_clamp_fusion.1) | copy-start | bytes 12292
  642.5 29.2 %all-to-all-start.4 = ((bf16[32,1,2]{2,1,0:T(2,128)(2,1)}), bf16[32,1,2]{2,1,0:T(2,128)(2,1)S(1)}, u32[]{:S(2)}, u32[]{:S(2)}) async-start(bf16[32,1,2]{2,1,0:T(2,128)(2,1)} %broadcast_select_fusion.13), calls=%async_computation.4 | async-start | bytes 32768 | tf_op jit(solution)/shard_map/all_to_all | solution.py:92
  671.6 10.1 copy-start.8
  671.6 106.2 %all-to-all-start.3 = ((bf16[32,2,128,2,128]{4,2,3,1,0:T(8,128)(2,1)}), bf16[32,2,128,2,128]{4,2,3,1,0:T(8,128)(2,1)}, u32[]{:S(2)}, u32[]{:S(2)}) async-start(bf16[32,2,128,2,128]{4,2,3,1,0:T(8,128)(2,1)} %broadcast_select_fusion.2), calls=%async_computation.3 | async-start | bytes 8388608 | tf_op jit(solution)/shard_map/all_to_all | solution.py:91
  681.7 71.3 %all-gather.11.cloned.1.call-start = ((), (), s32[]{:S(2)}) async-start(), calls=%async_computation.9 | async-start | bytes 3538944 | tf_op jit(solution)/shard_map/all_gather | solution.py:105
  682.3 75.3 %copy-start.32 = (bf16[1,64,128]{2,1,0:T(8,128)(2,1)S(1)}, bf16[1,64,128]{2,1,0:T(8,128)(2,1)}, u32[]{:S(2)}) copy-start(bf16[1,64,128]{2,1,0:T(8,128)(2,1)} %get-tuple-element.154) | copy-start | bytes 49156
  684.0 68.9 %copy-start.45 = (pred[32]{0:T(512)(128)(4,1)}, pred[32]{0:T(512)(128)(4,1)S(1)}, u32[]{:S(2)}) copy-start(pred[32]{0:T(512)(128)(4,1)S(1)} %iota_compare_fusion.9) | copy-start | bytes 100
  684.0 68.9 %copy-start.43 = (s32[1024]{0:T(1024)}, s32[1024]{0:T(1024)S(1)}, u32[]{:S(2)}) copy-start(s32[1024]{0:T(1024)S(1)} %pad_clamp_fusion) | copy-start | bytes 12292
  757.9 28.3 %copy-start.38 = (s32[2]{0:T(128)S(1)}, s32[2]{0:T(128)}, u32[]{:S(2)}) copy-start(s32[2]{0:T(128)} %copy-done.37) | copy-start | bytes 28
  777.9 32.4 %all-to-all-start.6 = ((bf16[32,1,2]{2,1,0:T(2,128)(2,1)}), bf16[32,1,2]{2,1,0:T(2,128)(2,1)S(1)}, u32[]{:S(2)}, u32[]{:S(2)}) async-start(bf16[32,1,2]{2,1,0:T(2,128)(2,1)} %broadcast_select_fusion.12), calls=%async_computation.6 | async-start | bytes 32768 | tf_op jit(solution)/shard_map/all_to_all | solution.py:92
  788.3 19.6 %copy-start.48 = (pred[32]{0:T(512)(128)(4,1)S(1)}, pred[32]{0:T(512)(128)(4,1)}, u32[]{:S(2)}) copy-start(pred[32]{0:T(512)(128)(4,1)} %copy-done.47) | copy-start | bytes 100
  810.2 10.7 copy-start.7
  810.8 106.2 %all-to-all-start.5 = ((bf16[32,2,128,2,128]{4,2,3,1,0:T(8,128)(2,1)}), bf16[32,2,128,2,128]{4,2,3,1,0:T(8,128)(2,1)}, u32[]{:S(2)}, u32[]{:S(2)}) async-start(bf16[32,2,128,2,128]{4,2,3,1,0:T(8,128)(2,1)} %broadcast_select_fusion.1), calls=%async_computation.5 | async-start | bytes 8388608 | tf_op jit(solution)/shard_map/all_to_all | solution.py:91
  820.8 71.1 %all-gather.13.cloned.1.call-start = ((), (), s32[]{:S(2)}) async-start(), calls=%async_computation.10 | async-start | bytes 3538944 | tf_op jit(solution)/shard_map/all_gather | solution.py:105
  822.4 129.0 %all-gather.15.cloned.1.call-start = ((), (), s32[]{:S(2)}) async-start(), calls=%async_computation.11 | async-start | bytes 3538944 | tf_op jit(solution)/shard_map/all_gather | solution.py:105
  829.4 66.1 %copy-start.28 = (f32[64,6]{0,1:T(8,128)S(1)}, f32[64,6]{0,1:T(8,128)}, u32[]{:S(2)}) copy-start(f32[64,6]{0,1:T(8,128)} %get-tuple-element.208) | copy-start | bytes 4612
  830.0 65.7 %copy-start.20 = (bf16[64,6]{1,0:T(8,128)(2,1)S(1)}, bf16[64,6]{1,0:T(8,128)(2,1)}, u32[]{:S(2)}) copy-start(bf16[64,6]{1,0:T(8,128)(2,1)} %copy.116) | copy-start | bytes 2308
  830.0 66.0 %copy-start.31 = (bf16[1,64,128]{2,1,0:T(8,128)(2,1)S(1)}, bf16[1,64,128]{2,1,0:T(8,128)(2,1)}, u32[]{:S(2)}) copy-start(bf16[1,64,128]{2,1,0:T(8,128)(2,1)} %get-tuple-element.155) | copy-start | bytes 49156
  830.0 66.0 %copy-start.16 = (bf16[64,2,128]{2,0,1:T(8,128)(2,1)S(1)}, bf16[64,2,128]{2,0,1:T(8,128)(2,1)}, u32[]{:S(2)}) copy-start(bf16[64,2,128]{2,0,1:T(8,128)(2,1)} %copy-done.15) | copy-start | bytes 98308
  830.0 66.2 %copy-start.22 = (bf16[64,1,128]{2,0,1:T(8,128)(2,1)S(1)}, bf16[64,1,128]{2,0,1:T(8,128)(2,1)}, u32[]{:S(2)}) copy-start(bf16[64,1,128]{2,0,1:T(8,128)(2,1)} %slice.517) | copy-start | bytes 49156
  896.3 21.7 %copy-start.40 = (s32[2]{0:T(128)S(1)}, s32[2]{0:T(128)}, u32[]{:S(2)}) copy-start(s32[2]{0:T(128)} %copy-done.39) | copy-start | bytes 28
  920.0 19.8 %copy-start.46 = (pred[32]{0:T(512)(128)(4,1)S(1)}, pred[32]{0:T(512)(128)(4,1)}, u32[]{:S(2)}) copy-start(pred[32]{0:T(512)(128)(4,1)} %copy-done.45) | copy-start | bytes 100
  942.2 8.9 copy-start.12
  942.2 103.8 %all-to-all-start.7 = ((bf16[32,2,128,2,128]{4,2,3,1,0:T(8,128)(2,1)}), bf16[32,2,128,2,128]{4,2,3,1,0:T(8,128)(2,1)}, u32[]{:S(2)}, u32[]{:S(2)}) async-start(bf16[32,2,128,2,128]{4,2,3,1,0:T(8,128)(2,1)} %broadcast_select_fusion), calls=%async_computation.7 | async-start | bytes 8388608 | tf_op jit(solution)/shard_map/all_to_all | solution.py:91
  956.3 10.0 copy-start.25
  970.9 10.0 copy-start.24
  997.7 49.2 %copy-start.36 = (s32[2]{0:T(128)S(1)}, s32[2]{0:T(128)}, u32[]{:S(2)}) copy-start(s32[2]{0:T(128)} %copy-done.35) | copy-start | bytes 28
  (18 other events, 97.7 us)
Sparse Core Ops, SparseCore 0:
  68.6 289.8 all-reduce.9
  361.4 233.7 all-reduce.7
  597.0 41.1 all-gather.8
  684.0 68.9 all-gather.10
  823.1 68.7 all-gather.12
  893.6 47.7 all-gather.14
